TPU v7x, 32 devices: a whole 2x2x4 slice. The times are simulated.
32 devices in a mesh: seq: 4 (over z), head: 8 (over y, x, core).
Axes of the slice: x: 2, y: 2, z: 4, core: 2. Of those that a mesh axis runs over, the one named last changes fastest.
Arguments:
- inputs: bfloat16 [2048, 8192], P('seq'), may hold values from -6 to 6
- w_qkv: bfloat16 [3, 8192, 2048], P(None, None, 'head'), may hold values from -0.0625 to 0.0625
- w_out: bfloat16 [2048, 8192], P('head'), may hold values from -0.1875 to 0.1875
- turn_ids: int32 [4, 512], P('seq'), may hold values from 0 to 15, never falling along the last dimension, each value on 1 to 64 neighbouring positions
- picked: int32 [4, 64], P('seq'), may hold values from 0 to 511
- owners: int32 [256, 1], P('seq'), may hold values from 0 to 7; in each aligned block of 64 rows (0 to 63, 64 to 127, ...) at most 32 rows name the same one
- candidates: bfloat16 [2048, 8192], P(('seq', 'head')), may hold values from -0.25 to 0.25
Outputs:
- mixed: bfloat16 [2048, 8192], P('seq', 'head')
- scores: float32 [1024, 64], P(('seq', 'head'))
Inputs may be any that keep to these rules, and one draw needn't show every extreme that they name: `turn_ids`: within each session turn numbers start at 0, never fall, and each turn has 1 to 64 tokens. `owners`: among the 64 picked rows of one session no owner is named more than 32 times.
All inputs are finite; a program needn't handle non-finite values.
Results may differ from a plain program's by a relative error of at most 0.008.
Values may be sent and summed in bfloat16 or wider, within the bound.
No kernel may reach another device: no remote copies, remote signals or barrier semaphores. Data moves between devices by JAX's collectives and lax.ppermute only.
A program may use at most 128 MiB of HBM per device.

v0:
```python
import jax
import jax.numpy as jnp
from jax import lax
from jax.sharding import PartitionSpec as P

HDIM = 128


def carried_in(value, axis, join, neutral):
    count, mine = (lax.axis_size(axis), lax.axis_index(axis))
    pieces = lax.all_gather(value, axis)
    so_far = jnp.full_like(value, 0) + jnp.asarray(neutral, value.dtype)

    def lap(position, so_far):
        longer = join(so_far, pieces[position])
        return jnp.where(position < mine, longer, so_far)

    return lax.fori_loop(0, count - 1, lap, so_far)


def per_device(inputs, w_qkv, w_out, turn_ids, picked, owners, candidates):
    tokens_here = inputs.shape[0]
    model_width = inputs.shape[1]
    heads_here = w_qkv.shape[2] // HDIM
    n_head = lax.axis_size("head")
    col_count = model_width // n_head
    projected = lax.dot_general(
        inputs, w_qkv, (((1,), (1,)), ((), ())), preferred_element_type=jnp.float32
    ).astype(jnp.bfloat16)
    query = projected[:, 0].reshape(tokens_here, heads_here, HDIM)
    keys = projected[:, 1].reshape(tokens_here, heads_here, HDIM)
    values = projected[:, 2].reshape(tokens_here, heads_here, HDIM)
    states = jnp.einsum("thi,thj->hij", keys, values, preferred_element_type=jnp.float32)
    prefix = carried_in(states, "seq", jnp.add, jnp.zeros_like(states))
    prefix = prefix.astype(jnp.bfloat16)
    scores_local = jnp.einsum("thi,shi->hts", query, keys, preferred_element_type=jnp.float32)
    tok_pos = jnp.arange(tokens_here, dtype=jnp.int32)
    causal = tok_pos[:, None] >= tok_pos[None, :]
    weights = jnp.where(causal[None, :, :], scores_local, 0.0).astype(jnp.bfloat16)
    local_part = jnp.einsum("hts,shj->thj", weights, values, preferred_element_type=jnp.float32)
    carried = jnp.einsum("thi,hij->thj", query, prefix, preferred_element_type=jnp.float32)
    summed = local_part + carried
    normed = summed * lax.rsqrt(jnp.mean(summed * summed, axis=-1, keepdims=True) + 1e-05)
    attended = normed.astype(jnp.bfloat16).reshape(tokens_here, heads_here * HDIM)
    input_cols = lax.dynamic_slice_in_dim(inputs, lax.axis_index("head") * col_count, col_count, 1)
    w_cols = lax.all_to_all(w_out, "head", split_axis=1, concat_axis=0, tiled=True)
    branch = jnp.dot(
        lax.all_gather(attended, "head", axis=1, tiled=True),
        w_cols,
        preferred_element_type=jnp.float32,
    )
    mixed = (input_cols.astype(jnp.float32) + branch).astype(jnp.bfloat16)
    turn_row = turn_ids[0]
    pick_row = picked[0]
    r_dev = pick_row.shape[0]
    cap_rows = 4 * r_dev // n_head
    pick_hot = tok_pos[None, :] == pick_row[:, None]
    sel_turn = jnp.sum(jnp.where(pick_hot, turn_row[None, :], 0), axis=1)
    member = (turn_row[None, :] == sel_turn[:, None]) & (tok_pos[None, :] <= pick_row[:, None])
    row_count = jnp.sum(member.astype(jnp.float32), axis=1)
    pooled = jnp.dot(member.astype(jnp.bfloat16), mixed, preferred_element_type=jnp.float32)
    summary = (pooled / row_count[:, None]).astype(jnp.bfloat16)
    owner_row = owners[:, 0]
    row_pos = jnp.arange(r_dev, dtype=jnp.int32)
    head_pos = jnp.arange(n_head, dtype=jnp.int32)
    own_hot = (owner_row[:, None] == head_pos[None, :]).astype(jnp.int32)
    before = (row_pos[:, None] > row_pos[None, :]).astype(jnp.int32)
    slot_rank = jnp.sum(jnp.dot(before, own_hot) * own_hot, axis=1)
    slot_index = owner_row * cap_rows + slot_rank
    dispatch = (
        slot_index[None, :] == jnp.arange(n_head * cap_rows, dtype=jnp.int32)[:, None]
    ).astype(jnp.bfloat16)
    outgoing = jnp.dot(dispatch, summary, preferred_element_type=jnp.float32).astype(jnp.bfloat16)
    outgoing = outgoing.reshape(n_head, cap_rows, col_count)
    cand_parts = candidates.reshape(candidates.shape[0], n_head, col_count)
    scores = jnp.einsum(
        "skc,nsc->kn",
        lax.all_to_all(outgoing, "head", split_axis=0, concat_axis=0, tiled=True),
        cand_parts,
        preferred_element_type=jnp.float32,
    )
    return (mixed, scores)


def solution(mesh):
    return jax.shard_map(
        per_device,
        mesh=mesh,
        in_specs=(
            P("seq", None),
            P(None, None, "head"),
            P("head", None),
            P("seq", None),
            P("seq", None),
            P("seq", None),
            P(("seq", "head"), None),
        ),
        out_specs=(P("seq", "head"), P(("seq", "head"), None)),
        check_vma=False,
    )
```

profile of v0, /device:TPU:0, one launch (start us, length us, event | category | flops | bytes accessed | tf_op | source)
XLA Modules:
  0.0 109.3 jit_solution(5474585538032914516)
XLA Ops:
  7.2 6.4 %copy.43 = bf16[256,8192]{0,1:T(8,128)(2,1)} copy(bf16[256,8192]{1,0:T(8,128)(2,1)} %param.11) | data formatting | bytes 8388608 | tf_op args[2]
  13.6 5.2 %all-to-all-start = ((bf16[256,8,1024]{0,2,1:T(8,128)(2,1)}), bf16[256,8,1024]{0,2,1:T(8,128)(2,1)}, u32[]{:S(2)}, u32[]{:S(2)}) async-start(bf16[256,8,1024]{0,2,1:T(8,128)(2,1)} %bitcast.41), calls=%async_computation | async-start | bytes 8388608 | tf_op jit(solution)/shard_map/all_to_all | solution.py:46
  18.8 0.0 all-gather.3.cloned.1.call-start
  18.8 0.1 iota_compare_fusion
  18.9 12.2 %fusion.2 = bf16[512,3,256]{0,2,1:T(8,128)(2,1)S(1)} fusion(bf16[3,8192,256]{2,1,0:T(8,128)(2,1)} %param.10, bf16[512,8192]{1,0:T(8,128)(2,1)} %param.9), kind=kOutput, calls=%fused_computation.5 | convolution fusion | flops 6442844160 | bytes 21757952 | tf_op jit(solution)/shard_map/dot_general | solution.py:27
  31.1 0.1 fusion.29
  31.2 0.2 fusion.30
  31.4 17.1 %all-gather = f32[8,128,128]{2,1,0:T(8,128)S(1)} all-gather(f32[2,128,128]{2,1,0:T(8,128)S(1)} %fusion.30), channel_id=2, replica_groups=mesh['seq'=4,'head'=8] {'seq'}, dimensions={0}, use_global_device_ids=true | all-gather | bytes 655360 | tf_op jit(solution)/shard_map/all_gather | solution.py:11
  48.5 0.2 while.14
  48.7 0.3 fusion.23
  49.0 0.8 multiply_reduce_fusion
  49.8 0.7 multiply_convert_fusion
  50.5 0.0 all-gather.3.cloned.1.call-update
  50.6 0.1 fusion.9
  50.7 0.2 select_reduce_fusion
  50.9 0.2 convert_reduce_fusion
  51.1 19.6 %all-to-all-done = bf16[256,8,1024]{0,2,1:T(8,128)(2,1)} async-done(((bf16[256,8,1024]{0,2,1:T(8,128)(2,1)}), bf16[256,8,1024]{0,2,1:T(8,128)(2,1)}, u32[]{:S(2)}, u32[]{:S(2)}) %all-to-all-start) | async-done | bytes 4194336 | tf_op jit(solution)/shard_map/all_to_all | solution.py:46
  70.8 6.5 %copy.44 = bf16[8,256,1024]{2,1,0:T(8,128)(2,1)} copy(bf16[8,256,1024]{1,2,0:T(8,128)(2,1)} %bitcast.8) | data formatting | bytes 8388608 | tf_op jit(solution)/shard_map/all_to_all | solution.py:46
  77.2 5.9 %all-gather.3.cloned.1.call-done = bf16[512,2048]{0,1:T(8,128)(2,1)} async-done(((bf16[512,256]{0,1:T(8,128)(2,1)}), bf16[512,2048]{0,1:T(8,128)(2,1)}) %all-gather.3.cloned.1.call-update) | async-done | bytes 2097168 | tf_op jit(solution)/shard_map/all_gather | solution.py:48
  83.1 5.5 %add_convert_fusion = bf16[512,1024]{1,0:T(8,128)(2,1)S(1)} fusion(bf16[512,2048]{0,1:T(8,128)(2,1)} %all-gather.3.cloned.1.call-done, bf16[2048,1024]{1,0:T(8,128)(2,1)} %bitcast.42, bf16[512,8192]{1,0:T(8,128)(2,1)} %param.9, s32[]{:T(128)S(6)} %select_n.32), kind=kOutput, calls=%fused_computation.3 | convolution fusion | flops 2149056512 | bytes 8388612 | tf_op jit(solution)/shard_map/dot_general | solution.py:47
  88.6 0.0 copy-start.4
  88.6 0.5 convolution_convert_fusion
  89.2 12.3 %all_to_all.24 = bf16[8,32,1024]{2,1,0:T(8,128)(2,1)S(1)} all-to-all(bf16[8,32,1024]{2,1,0:T(8,128)(2,1)S(1)} %bitcast.51), channel_id=1, replica_groups=mesh['seq'=4,'head'=8] {'head'}, dimensions={0} | all-to-all | bytes 1048576 | tf_op jit(solution)/shard_map/all_to_all | solution.py:78
  101.4 1.0 convolution_bitcast_fusion
  (15 shorter events, 0.2 us)
Async XLA Ops:
  13.6 57.2 %all-to-all-start = ((bf16[256,8,1024]{0,2,1:T(8,128)(2,1)}), bf16[256,8,1024]{0,2,1:T(8,128)(2,1)}, u32[]{:S(2)}, u32[]{:S(2)}) async-start(bf16[256,8,1024]{0,2,1:T(8,128)(2,1)} %bitcast.41), calls=%async_computation | async-start | bytes 8388608 | tf_op jit(solution)/shard_map/all_to_all | solution.py:46
  18.8 64.3 %all-gather.3.cloned.1.call-start = ((), (), s32[]{:S(2)}) async-start(), calls=%async_computation.2 | async-start | bytes 2359296 | tf_op jit(solution)/shard_map/all_gather | solution.py:48
  31.1 19.4 %copy-start.3 = (s32[64,1]{0,1:T(1,128)S(1)}, s32[64,1]{0,1:T(1,128)}, u32[]{:S(2)}) copy-start(s32[64,1]{0,1:T(1,128)} %param.14) | copy-start | bytes 772
  31.1 19.6 %copy-start = (s32[1,512]{1,0:T(1,128)S(1)}, s32[1,512]{1,0:T(1,128)}, u32[]{:S(2)}) copy-start(s32[1,512]{1,0:T(1,128)} %param.12) | copy-start | bytes 6148
  31.2 19.6 %copy-start.1 = (s32[1,64]{1,0:T(1,128)S(1)}, s32[1,64]{1,0:T(1,128)}, u32[]{:S(2)}) copy-start(s32[1,64]{1,0:T(1,128)} %param.13) | copy-start | bytes 772
  83.1 18.3 %copy-start.2 = (bf16[64,8192]{1,0:T(8,128)(2,1)S(1)}, bf16[64,8192]{1,0:T(8,128)(2,1)}, u32[]{:S(2)}) copy-start(bf16[64,8192]{1,0:T(8,128)(2,1)} %param.15) | copy-start | bytes 3145732
  88.6 13.8 %copy-start.4 = (bf16[512,1024]{1,0:T(8,128)(2,1)}, bf16[512,1024]{1,0:T(8,128)(2,1)S(1)}, u32[]{:S(2)}) copy-start(bf16[512,1024]{1,0:T(8,128)(2,1)S(1)} %add_convert_fusion) | copy-start | bytes 3145732
Sparse Core Ops, SparseCore 0:
  50.7 32.3 all-gather.2
where the time goes:
time: 110 us; the launch traced here: 109 us
  blocking collectives  29.4 us (27%)
  waiting for transfers between devices  25.5 us (23%)
  matrix products  20.7 us (19%)
  between operations  14.2 us (13%)
  local copies, waits for them, and re-layouts  13 us (12%)
  starting transfers between devices  5.23 us (5%)
  other arithmetic  1.34 us (1%)
    all_to_all x1, waiting for transfers between devices, per_device(): lax.all_to_all(w_out, 'head', split_axis=1, concat_axis=0, tiled=True)  19.6 us
    all_gather x1, blocking collectives, carried_in(): pieces = lax.all_gather(value, axis)  17.1 us
    all_to_all x1, blocking collectives, per_device(): lax.all_to_all(outgoing, 'head', split_axis=0, concat_axis=0, tiled=True)  12.3 us
    dot_general x1, matrix products, per_device(): lax.dot_general(inputs, w_qkv, (((1,), (1,)), ((), ())), preferred_elemen...  12.2 us
    all_to_all x1, local copies, waits for them, and re-layouts, per_device(): lax.all_to_all(w_out, 'head', split_axis=1, concat_axis=0, tiled=True)  6.48 us
    unnamed x11, local copies, waits for them, and re-layouts  6.43 us
    all_gather x1, waiting for transfers between devices, per_device(): lax.all_gather(attended, 'head', axis=1, tiled=True)  5.86 us
    dot_general x1, matrix products, per_device(): jnp.dot(lax.all_gather(attended, 'head', axis=1, tiled=True), w_cols, pre...  5.52 us
  transfers between devices with their start and end apart: 2, of which 2 were waited for; matrix products, arithmetic and copies ran while one was open for 20% of the time, Pallas kernels for 0%

commit v1 on v0

--- a/solution.py
+++ b/solution.py
@@ -43,7 +43,10 @@
     normed = summed * lax.rsqrt(jnp.mean(summed * summed, axis=-1, keepdims=True) + 1e-05)
     attended = normed.astype(jnp.bfloat16).reshape(tokens_here, heads_here * HDIM)
     input_cols = lax.dynamic_slice_in_dim(inputs, lax.axis_index("head") * col_count, col_count, 1)
-    w_cols = lax.all_to_all(w_out, "head", split_axis=1, concat_axis=0, tiled=True)
+    w_cols = jnp.concatenate(
+        lax.all_to_all(jnp.stack(jnp.split(w_out, lax.axis_size("head"), axis=1)), "head", 0, 0),
+        axis=0,
+    )
     branch = jnp.dot(
         lax.all_gather(attended, "head", axis=1, tiled=True),
         w_cols,

time: 110 us -> 140 us (1.27)
  waiting for transfers between devices: 25.5 us -> 53.8 us
  local copies, waits for them, and re-layouts: 13 us -> 15.2 us
    all_to_all x1, waiting for transfers between devices: 19.6 us -> 39 us  [per_device(): lax.all_to_all(jnp.stack(jnp.split(w_out, lax.axis_size('head'), axis=1))...]
    all_gather x1, waiting for transfers between devices: 5.86 us -> 14.8 us  [per_device(): lax.all_gather(attended, 'head', axis=1, tiled=True)]
    unnamed x11 -> x17, local copies, waits for them, and re-layouts: 6.43 us -> 13.2 us
    all_to_all x1 -> x0, local copies, waits for them, and re-layouts: 6.48 us -> none  [per_device(): lax.all_to_all(w_out, 'head', split_axis=1, concat_axis=0, tiled=True)]
    another operation x0 -> x1, local copies, waits for them, and re-layouts: none -> 1.89 us  [per_device(): jnp.stack(jnp.split(w_out, lax.axis_size('head'), axis=1))]
  transfers between devices with their start and end apart: 2 -> 2, of which waited for: 2 -> 2; matrix products, arithmetic and copies ran while one was open for 20% -> 11% of each run, Pallas kernels for 0% -> 0%
where the time goes in v1:
time: 140 us; the launch traced here: 139 us
  waiting for transfers between devices  53.8 us (38%)
  blocking collectives  29.5 us (21%)
  matrix products  20.6 us (15%)
  local copies, waits for them, and re-layouts  15.2 us (11%)
  between operations  14.2 us (10%)
  starting transfers between devices  4.7 us (3%)
    all_to_all x1, waiting for transfers between devices, per_device(): lax.all_to_all(jnp.stack(jnp.split(w_out, lax.axis_size('head'), axis=1))...  39 us
    all_gather x1, blocking collectives, carried_in(): pieces = lax.all_gather(value, axis)  17.4 us
    all_gather x1, waiting for transfers between devices, per_device(): lax.all_gather(attended, 'head', axis=1, tiled=True)  14.8 us
    unnamed x17, local copies, waits for them, and re-layouts  13.2 us
    dot_general x1, matrix products, per_device(): lax.dot_general(inputs, w_qkv, (((1,), (1,)), ((), ())), preferred_elemen...  12.2 us
    all_to_all x1, blocking collectives, per_device(): lax.all_to_all(outgoing, 'head', split_axis=0, concat_axis=0, tiled=True)  12.1 us
    dot_general x1, matrix products, per_device(): jnp.dot(lax.all_gather(attended, 'head', axis=1, tiled=True), w_cols, pre...  5.52 us
    all_to_all x1, starting transfers between devices, per_device(): lax.all_to_all(jnp.stack(jnp.split(w_out, lax.axis_size('head'), axis=1))...  4.67 us
  transfers between devices with their start and end apart: 2, of which 2 were waited for; matrix products, arithmetic and copies ran while one was open for 11% of the time, Pallas kernels for 0%

profile of v1, /device:TPU:0, one launch (start us, length us, event | category | flops | bytes accessed | tf_op | source)
XLA Modules:
  0.0 139.4 jit_solution(8883536109682802164)
XLA Ops:
  7.3 12.2 %fusion.2 = bf16[512,3,256]{0,2,1:T(8,128)(2,1)S(1)} fusion(bf16[3,8192,256]{2,1,0:T(8,128)(2,1)} %param.10, bf16[512,8192]{1,0:T(8,128)(2,1)} %param.9), kind=kOutput, calls=%fused_computation.5 | convolution fusion | flops 6442844160 | bytes 21757952 | tf_op jit(solution)/shard_map/dot_general | solution.py:27
  19.5 0.2 fusion.30
  19.8 17.4 %all-gather = f32[8,128,128]{2,1,0:T(8,128)S(1)} all-gather(f32[2,128,128]{2,1,0:T(8,128)S(1)} %fusion.30), channel_id=2, replica_groups=mesh['seq'=4,'head'=8] {'seq'}, dimensions={0}, use_global_device_ids=true | all-gather | bytes 655360 | tf_op jit(solution)/shard_map/all_gather | solution.py:11
  37.1 0.2 while.14
  37.3 0.3 fusion.23
  37.6 0.8 multiply_reduce_fusion
  38.4 0.7 multiply_convert_fusion
  39.2 1.9 %bitcast_dynamic-update-slice_fusion.7 = bf16[8,256,1024]{2,1,0:T(8,128)(2,1)} fusion(bf16[256,8192]{1,0:T(8,128)(2,1)} %param.11), kind=kLoop, calls=%fused_computation.27 | loop fusion | bytes 1048576
  41.1 1.9 %bitcast_dynamic-update-slice_fusion.6 = bf16[8,256,1024]{2,1,0:T(8,128)(2,1)} fusion(bf16[8,256,1024]{2,1,0:T(8,128)(2,1)} %bitcast_dynamic-update-slice_fusion.7, bf16[256,8192]{1,0:T(8,128)(2,1)} %param.11), kind=kLoop, calls=%fused_computation.26 | loop fusion | bytes 1048576
  42.9 1.9 %bitcast_dynamic-update-slice_fusion.5 = bf16[8,256,1024]{2,1,0:T(8,128)(2,1)} fusion(bf16[8,256,1024]{2,1,0:T(8,128)(2,1)} %bitcast_dynamic-update-slice_fusion.6, bf16[256,8192]{1,0:T(8,128)(2,1)} %param.11), kind=kLoop, calls=%fused_computation.25 | loop fusion | bytes 1048576
  44.8 1.9 %bitcast_dynamic-update-slice_fusion.4 = bf16[8,256,1024]{2,1,0:T(8,128)(2,1)} fusion(bf16[8,256,1024]{2,1,0:T(8,128)(2,1)} %bitcast_dynamic-update-slice_fusion.5, bf16[256,8192]{1,0:T(8,128)(2,1)} %param.11), kind=kLoop, calls=%fused_computation.24 | loop fusion | bytes 1048576
  46.7 1.9 %bitcast_dynamic-update-slice_fusion.3 = bf16[8,256,1024]{2,1,0:T(8,128)(2,1)} fusion(bf16[8,256,1024]{2,1,0:T(8,128)(2,1)} %bitcast_dynamic-update-slice_fusion.4, bf16[256,8192]{1,0:T(8,128)(2,1)} %param.11), kind=kLoop, calls=%fused_computation.23 | loop fusion | bytes 1048576
  48.6 1.9 %bitcast_dynamic-update-slice_fusion.2 = bf16[8,256,1024]{2,1,0:T(8,128)(2,1)} fusion(bf16[8,256,1024]{2,1,0:T(8,128)(2,1)} %bitcast_dynamic-update-slice_fusion.3, bf16[256,8192]{1,0:T(8,128)(2,1)} %param.11), kind=kLoop, calls=%fused_computation.22 | loop fusion | bytes 1048576
  50.5 1.9 %bitcast_dynamic-update-slice_fusion.1 = bf16[8,256,1024]{2,1,0:T(8,128)(2,1)} fusion(bf16[8,256,1024]{2,1,0:T(8,128)(2,1)} %bitcast_dynamic-update-slice_fusion.2, bf16[256,8192]{1,0:T(8,128)(2,1)} %param.11), kind=kLoop, calls=%fused_computation.21 | loop fusion | bytes 1048576
  52.4 1.9 %bitcast_dynamic-update-slice_fusion = bf16[8,256,1024]{2,1,0:T(8,128)(2,1)} fusion(bf16[8,256,1024]{2,1,0:T(8,128)(2,1)} %bitcast_dynamic-update-slice_fusion.1, bf16[256,8192]{1,0:T(8,128)(2,1)} %param.11), kind=kLoop, calls=%fused_computation.20 | loop fusion | bytes 1048576 | tf_op jit(solution)/shard_map/stack | solution.py:47
  54.3 4.7 %all-to-all-start = ((bf16[8,256,1024]{2,1,0:T(8,128)(2,1)}), bf16[8,256,1024]{2,1,0:T(8,128)(2,1)}, u32[]{:S(2)}, u32[]{:S(2)}) async-start(bf16[8,256,1024]{2,1,0:T(8,128)(2,1)} %bitcast_dynamic-update-slice_fusion), calls=%async_computation | async-start | bytes 8388608 | tf_op jit(solution)/shard_map/all_to_all | solution.py:47
  59.1 0.2 select_reduce_fusion
  59.3 0.2 convert_reduce_fusion
  59.5 14.8 %all-gather.3.cloned.1.call-done = bf16[512,2048]{0,1:T(8,128)(2,1)} async-done(((bf16[512,256]{0,1:T(8,128)(2,1)}), bf16[512,2048]{0,1:T(8,128)(2,1)}) %all-gather.3.cloned.1.call-update) | async-done | bytes 2097168 | tf_op jit(solution)/shard_map/all_gather | solution.py:51
  74.4 39.0 %all-to-all-done = bf16[8,256,1024]{2,1,0:T(8,128)(2,1)} async-done(((bf16[8,256,1024]{2,1,0:T(8,128)(2,1)}), bf16[8,256,1024]{2,1,0:T(8,128)(2,1)}, u32[]{:S(2)}, u32[]{:S(2)}) %all-to-all-start) | async-done | bytes 4194336 | tf_op jit(solution)/shard_map/all_to_all | solution.py:47
  113.3 5.5 %add_convert_fusion = bf16[512,1024]{1,0:T(8,128)(2,1)S(1)} fusion(bf16[512,2048]{0,1:T(8,128)(2,1)} %all-gather.3.cloned.1.call-done, bf16[2048,1024]{1,0:T(8,128)(2,1)} %bitcast.15, bf16[512,8192]{1,0:T(8,128)(2,1)} %param.9, s32[]{:T(128)S(6)} %select_n.32), kind=kOutput, calls=%fused_computation.3 | convolution fusion | flops 2149056512 | bytes 8388612 | tf_op jit(solution)/shard_map/dot_general | solution.py:50
  118.9 0.5 convolution_convert_fusion
  119.4 12.1 %all_to_all.10 = bf16[8,32,1024]{2,1,0:T(8,128)(2,1)S(1)} all-to-all(bf16[8,32,1024]{2,1,0:T(8,128)(2,1)S(1)} %bitcast.63), channel_id=1, replica_groups=mesh['seq'=4,'head'=8] {'head'}, dimensions={0} | all-to-all | bytes 1048576 | tf_op jit(solution)/shard_map/all_to_all | solution.py:81
  131.5 1.0 convolution_bitcast_fusion
  (21 shorter events, 0.5 us)
Async XLA Ops:
  7.2 67.2 %all-gather.3.cloned.1.call-start = ((), (), s32[]{:S(2)}) async-start(), calls=%async_computation.2 | async-start | bytes 2359296 | tf_op jit(solution)/shard_map/all_gather | solution.py:51
  54.3 4.7 %copy-start.3 = (s32[64,1]{0,1:T(1,128)S(1)}, s32[64,1]{0,1:T(1,128)}, u32[]{:S(2)}) copy-start(s32[64,1]{0,1:T(1,128)} %param.14) | copy-start | bytes 772
  54.3 4.8 %copy-start = (s32[1,512]{1,0:T(1,128)S(1)}, s32[1,512]{1,0:T(1,128)}, u32[]{:S(2)}) copy-start(s32[1,512]{1,0:T(1,128)} %param.12) | copy-start | bytes 6148
  54.3 4.8 %copy-start.1 = (s32[1,64]{1,0:T(1,128)S(1)}, s32[1,64]{1,0:T(1,128)}, u32[]{:S(2)}) copy-start(s32[1,64]{1,0:T(1,128)} %param.13) | copy-start | bytes 772
  54.3 59.0 %all-to-all-start = ((bf16[8,256,1024]{2,1,0:T(8,128)(2,1)}), bf16[8,256,1024]{2,1,0:T(8,128)(2,1)}, u32[]{:S(2)}, u32[]{:S(2)}) async-start(bf16[8,256,1024]{2,1,0:T(8,128)(2,1)} %bitcast_dynamic-update-slice_fusion), calls=%async_computation | async-start | bytes 8388608 | tf_op jit(solution)/shard_map/all_to_all | solution.py:47
  113.3 18.2 %copy-start.2 = (bf16[64,8192]{1,0:T(8,128)(2,1)S(1)}, bf16[64,8192]{1,0:T(8,128)(2,1)}, u32[]{:S(2)}) copy-start(bf16[64,8192]{1,0:T(8,128)(2,1)} %param.15) | copy-start | bytes 3145732
  118.9 13.7 %copy-start.4 = (bf16[512,1024]{1,0:T(8,128)(2,1)}, bf16[512,1024]{1,0:T(8,128)(2,1)S(1)}, u32[]{:S(2)}) copy-start(bf16[512,1024]{1,0:T(8,128)(2,1)S(1)} %add_convert_fusion) | copy-start | bytes 3145732
Sparse Core Ops, SparseCore 0:
  39.3 35.0 all-gather.2
